TPU v7x, 512 devices: a whole 4x4x16 slice. The times are simulated.
512 devices in a mesh: grid: 32 (over x, y, core), band: 16 (over z).
Axes of the slice: x: 4, y: 4, z: 16, core: 2. Of those that a mesh axis runs over, the one named last changes fastest.
Arguments:
- orbitals: bfloat16 [32768, 512], P('grid', 'band'), may hold values from -6 to 6
- rotation: bfloat16 [512, 32768], P('grid', 'band'), may hold values from -0.25 to 0.25
Outputs:
- rotated: bfloat16 [32768, 32768], P('grid', 'band')
All inputs are finite; a program needn't handle non-finite values.
Results may differ from a plain program's by a relative error of at most 0.001.
Values may be sent and summed in bfloat16 or wider, within the bound.
No kernel may reach another device: no remote copies, remote signals or barrier semaphores. Data moves between devices by JAX's collectives and lax.ppermute only.
A program may use at most 64 MiB of HBM per device.

v0:
```python
import jax
import jax.numpy as jnp
from jax import lax
from jax.sharding import PartitionSpec as P


def on_device(orbitals, rotation):
    all_cols = lax.all_gather(orbitals, "band", axis=1, tiled=True)
    all_rows = lax.all_gather(rotation, "grid", axis=0, tiled=True)
    total = jnp.dot(all_cols, all_rows, preferred_element_type=jnp.float32)
    return total.astype(jnp.bfloat16)


def solution(mesh):
    in_specs = (P("grid", "band"), P("grid", "band"))
    out_specs = P("grid", "band")
    return jax.shard_map(
        on_device, mesh=mesh, in_specs=in_specs, out_specs=out_specs, check_vma=False
    )
```

profile of v0, /device:TPU:1, one launch (start us, length us, event | category | flops | bytes accessed | tf_op | source)
XLA Modules:
  0.0 158.6 jit_solution(7569212816232975436)
XLA Ops:
  6.5 0.0 all-gather.3.cloned.1.call-start
  6.5 0.7 all-gather.3.cloned.1.call-update
  7.3 0.0 all-gather.5.cloned.1.call-start
  7.3 0.7 all-gather.5.cloned.1.call-update
  8.0 68.3 %all-gather.3.cloned.1.call-done = bf16[1024,512]{0,1:T(8,128)(2,1)} async-done(((bf16[1024,32]{0,1:T(8,128)(2,1)}), bf16[1024,512]{0,1:T(8,128)(2,1)}) %all-gather.3.cloned.1.call-update) | async-done | bytes 1048592 | tf_op jit(solution)/shard_map/all_gather | solution.py:8
  76.3 69.1 %all-gather.5.cloned.1.call-done = bf16[512,2048]{1,0:T(8,128)(2,1)} async-done(((bf16[16,2048]{1,0:T(8,128)(2,1)}), bf16[512,2048]{1,0:T(8,128)(2,1)}) %all-gather.5.cloned.1.call-update) | async-done | bytes 2097168 | tf_op jit(solution)/shard_map/all_gather | solution.py:9
  145.4 6.3 %convolution_convert_fusion = bf16[1024,2048]{1,0:T(8,128)(2,1)} fusion(bf16[1024,512]{0,1:T(8,128)(2,1)} %all-gather.3.cloned.1.call-done, bf16[512,2048]{1,0:T(8,128)(2,1)} %all-gather.5.cloned.1.call-done), kind=kOutput, calls=%fused_computation | convolution fusion | flops 2149580800 | bytes 7340032 | tf_op jit(solution)/shard_map/dot_general | solution.py:10
Async XLA Ops:
  6.5 69.8 %all-gather.3.cloned.1.call-start = ((), (), s32[]{:S(2)}) async-start(), calls=%async_computation | async-start | bytes 1114112 | tf_op jit(solution)/shard_map/all_gather | solution.py:8
  7.3 138.2 %all-gather.5.cloned.1.call-start = ((), (), s32[]{:S(2)}) async-start(), calls=%async_computation.1 | async-start | bytes 2162688 | tf_op jit(solution)/shard_map/all_gather | solution.py:9
Sparse Core Ops, SparseCore 0:
  9.4 66.8 all-gather.2
  79.5 65.8 all-gather.4
where the time goes:
time: 159 us
  waiting for transfers between devices  139 us (87%)
  between operations  13.4 us (8%)
  matrix products  6.32 us (4%)
    all_gather x1, waiting for transfers between devices, on_device(): all_rows = lax.all_gather(rotation, 'grid', axis=0, tiled=True)  69.1 us
    all_gather x1, waiting for transfers between devices, on_device(): all_cols = lax.all_gather(orbitals, 'band', axis=1, tiled=True)  68.3 us
    dot_general x1, matrix products, on_device(): total = jnp.dot(all_cols, all_rows, preferred_element_type=jnp.float32)  6.32 us
  transfers between devices with their start and end apart: 2, of which 2 were waited for; matrix products, arithmetic and copies ran while one was open for 0% of the time, Pallas kernels for 0%

commit v1 on v0

--- a/solution.py
+++ b/solution.py
@@ -6,7 +6,11 @@
 
 def on_device(orbitals, rotation):
     all_cols = lax.all_gather(orbitals, "band", axis=1, tiled=True)
-    all_rows = lax.all_gather(rotation, "grid", axis=0, tiled=True)
+    devices = lax.axis_size("grid")
+    repeats = [devices if d == 0 else 1 for d in range(rotation.ndim)]
+    all_rows = lax.all_to_all(
+        jnp.tile(rotation, repeats), "grid", split_axis=0, concat_axis=0, tiled=True
+    )
     total = jnp.dot(all_cols, all_rows, preferred_element_type=jnp.float32)
     return total.astype(jnp.bfloat16)
 

time: 159 us -> 108 us (0.68)
  the two profiles are of different devices: /device:TPU:1 before, /device:TPU:2 now
where the time goes in v1:
time: 108 us; the launch traced here: 107 us
  waiting for transfers between devices  76.2 us (71%)
  between operations  13.4 us (12%)
  starting transfers between devices  9.66 us (9%)
  matrix products  5.62 us (5%)
  local copies, waits for them, and re-layouts  2.41 us (2%)
    all_gather x1, waiting for transfers between devices, on_device(): all_cols = lax.all_gather(orbitals, 'band', axis=1, tiled=True)  75.5 us
    all_to_all x1, starting transfers between devices, on_device(): lax.all_to_all(jnp.tile(rotation, repeats), 'grid', split_axis=0, concat_...  9.62 us
    dot_general x1, matrix products, on_device(): total = jnp.dot(all_cols, all_rows, preferred_element_type=jnp.float32)  5.62 us
    another operation x1, local copies, waits for them, and re-layouts, on_device(): jnp.tile(rotation, repeats)  2.41 us
  transfers between devices with their start and end apart: 2, of which 1 were waited for; matrix products, arithmetic and copies ran while one was open for 0% of the time, Pallas kernels for 0%

profile of v1, /device:TPU:2, one launch (start us, length us, event | category | flops | bytes accessed | tf_op | source)
XLA Modules:
  0.0 107.3 jit_solution(8150759165919480075)
XLA Ops:
  6.5 2.4 %tile.2 = bf16[32,16,2048]{2,1,0:T(8,128)(2,1)} broadcast(bf16[16,2048]{1,0:T(8,128)(2,1)} %param.3), dimensions={1,2} | broadcast | bytes 2162688 | tf_op jit(solution)/shard_map/tile | solution.py:12
  8.9 9.6 %all-to-all-start = ((bf16[32,16,2048]{2,1,0:T(8,128)(2,1)}), bf16[32,16,2048]{2,1,0:T(8,128)(2,1)S(1)}, u32[]{:S(2)}, u32[]{:S(2)}) async-start(bf16[32,16,2048]{2,1,0:T(8,128)(2,1)} %tile.2), calls=%async_computation | async-start | bytes 4194304 | tf_op jit(solution)/shard_map/all_to_all | solution.py:11
  18.6 0.0 all-gather.2.cloned.1.call-start
  18.6 0.7 all-gather.2.cloned.1.call-update
  19.3 75.5 %all-gather.2.cloned.1.call-done = bf16[1024,512]{0,1:T(8,128)(2,1)} async-done(((bf16[1024,32]{0,1:T(8,128)(2,1)}), bf16[1024,512]{0,1:T(8,128)(2,1)}) %all-gather.2.cloned.1.call-update) | async-done | bytes 1048592 | tf_op jit(solution)/shard_map/all_gather | solution.py:8
  94.8 0.0 all-to-all-done
  94.8 5.6 %convolution_convert_fusion = bf16[1024,2048]{1,0:T(8,128)(2,1)} fusion(bf16[1024,512]{0,1:T(8,128)(2,1)} %all-gather.2.cloned.1.call-done, bf16[512,2048]{1,0:T(8,128)(2,1)S(1)} %bitcast.3), kind=kOutput, calls=%fused_computation | convolution fusion | flops 2149580800 | bytes 7340032 | tf_op jit(solution)/shard_map/dot_general | solution.py:14
Async XLA Ops:
  8.9 85.9 %all-to-all-start = ((bf16[32,16,2048]{2,1,0:T(8,128)(2,1)}), bf16[32,16,2048]{2,1,0:T(8,128)(2,1)S(1)}, u32[]{:S(2)}, u32[]{:S(2)}) async-start(bf16[32,16,2048]{2,1,0:T(8,128)(2,1)} %tile.2), calls=%async_computation | async-start | bytes 4194304 | tf_op jit(solution)/shard_map/all_to_all | solution.py:11
  18.6 76.2 %all-gather.2.cloned.1.call-start = ((), (), s32[]{:S(2)}) async-start(), calls=%async_computation.1 | async-start | bytes 1114112 | tf_op jit(solution)/shard_map/all_gather | solution.py:8
Sparse Core Ops, SparseCore 0:
  21.5 73.2 all-gather.1
